TPU v7x, 1024 devices: a whole 4x4x32 slice. The times are simulated.
1024 devices in a mesh: section: 2 (over y_hi), dp: 8 (over x, core), expert: 64 (over z, y_lo).
Axes of the slice: x: 4, y: 4 (y_hi: 2, y_lo: 2; y = y_hi * 2 + y_lo), z: 32, core: 2. Of those that a mesh axis runs over, the one named last changes fastest.
Arguments:
- activations: bfloat16 [2, 4096, 4096], P('section', 'expert'), may hold values from -6 to 6
- routes: int32 [2, 4096, 8], P('section', 'expert'), may hold values from 0 to 63, all different within a row; in each aligned block of 64 rows (0 to 63, 64 to 127, ..., all dimensions but the last counted through in order) at most 8 rows name the same one
- gate_weights: float32 [2, 4096, 8], P('section', 'expert'), may hold values from 0.05 to 0.5
- norm_gain: bfloat16 [4096], replicated, may hold values from 0.099609375 to 1.8984375
- gate_up_weights: bfloat16 [64, 2, 1536, 4096], P('expert', None, 'dp'), may hold values from -0.09375 to 0.09375
- down_weights: bfloat16 [64, 1536, 4096], P('expert', None, 'dp'), may hold values from -0.15625 to 0.15625
Outputs:
- arrived: bfloat16 [2, 4096, 4096], P('section', 'expert', 'dp')
Inputs may be any that keep to these rules, and one draw needn't show every extreme that they name: `routes`: each token names 8 different experts. Among the 64 tokens of one device (aligned blocks of 64 tokens), no expert is named more than 8 times, and in some blocks one expert is named exactly 8 times.
All inputs are finite; a program needn't handle non-finite values.
Results may differ from a plain program's by a relative error of at most 0.005.
Values may be sent and summed in bfloat16 or wider, within the bound.
A program may use at most 32 MiB of HBM per device.

v0:
```python
import jax
import jax.numpy as jnp
from jax import lax
from jax.sharding import PartitionSpec as P


def passed_along(block, axis, distance):
    devices = range(lax.axis_size(axis))
    route = [((i - distance) % len(devices), i) for i in devices]
    return lax.ppermute(block, axis, route)


def body(activations, routes, gate_weights, norm_gain, gate_up_weights, down_weights):
    tokens_here = activations[0]
    token_count, feature_count = tokens_here.shape
    top_count = routes.shape[2]
    local_experts = gate_up_weights.shape[0]
    expert_devices = lax.axis_size("expert")
    dp_devices = lax.axis_size("dp")
    total_experts = local_experts * expert_devices
    window = max(1, token_count * top_count // (total_experts * dp_devices))
    capacity = window * dp_devices
    slice_width = feature_count // dp_devices
    dp_place = lax.axis_index("dp")
    widened = tokens_here.astype(jnp.float32)
    mean_square = jnp.mean(widened * widened, axis=-1, keepdims=True)
    normed = (widened * lax.rsqrt(mean_square + 1e-06) * norm_gain.astype(jnp.float32)).astype(
        jnp.bfloat16
    )
    flat_routes = routes[0].reshape(-1)
    experts_iota = jnp.arange(total_experts, dtype=jnp.int32)
    onehot = (flat_routes[:, None] == experts_iota[None, :]).astype(jnp.int32)
    slot_ranks = jnp.sum((jnp.cumsum(onehot, axis=0) - onehot) * onehot, axis=1)
    targets = flat_routes * capacity + slot_ranks
    contract_rows = (((0,), (0,)), ((), ()))
    local_rank = slot_ranks - dp_place * window
    inside = (local_rank >= 0) & (local_rank < window)
    local_target = jnp.where(inside, flat_routes * window + local_rank, -1)
    slot_iota = jnp.arange(total_experts * window, dtype=jnp.int32)
    matches = (local_target[:, None] == slot_iota[None, :]).reshape(
        token_count, top_count, total_experts * window
    )
    placing = jnp.any(matches, axis=1).astype(jnp.bfloat16)
    outgoing = lax.dot_general(placing, normed, contract_rows, preferred_element_type=jnp.float32)
    outgoing = outgoing.astype(jnp.bfloat16).reshape(total_experts, window, feature_count)
    arriving = lax.all_to_all(outgoing, "expert", split_axis=0, concat_axis=0, tiled=True)
    arriving = arriving.reshape(expert_devices, local_experts, window, feature_count)
    gate_up = jnp.einsum(
        "sekd,ejhd->jsekh",
        lax.all_gather(arriving, "dp", axis=2, tiled=True),
        gate_up_weights,
        preferred_element_type=jnp.float32,
    )
    hidden_act = (jax.nn.silu(gate_up[0]) * gate_up[1]).astype(jnp.bfloat16)
    summed = jnp.einsum(
        "sech,ehf->secf",
        lax.all_gather(hidden_act, "dp", axis=3, tiled=True),
        down_weights,
        preferred_element_type=jnp.float32,
    )
    expert_out = summed.astype(jnp.bfloat16)
    returned = lax.all_to_all(expert_out, "expert", split_axis=0, concat_axis=0, tiled=True)
    returned_flat = returned.reshape(total_experts * capacity, slice_width)
    picked = jnp.take(returned_flat, targets, axis=0).reshape(token_count, top_count, slice_width)
    branch = jnp.sum(picked.astype(jnp.float32) * gate_weights[0][:, :, None], axis=1)
    residual = lax.dynamic_slice_in_dim(widened, dp_place * slice_width, slice_width, 1)
    finished = (residual + branch).astype(jnp.bfloat16)
    arrived = passed_along(finished, "section", 1)
    return arrived[None]


def solution(mesh):
    placed = (
        P("section", "expert", None),
        P("section", "expert", None),
        P("section", "expert", None),
        P(),
        P("expert", None, "dp", None),
        P("expert", None, "dp"),
    )
    return jax.shard_map(
        body, mesh=mesh, in_specs=placed, out_specs=P("section", "expert", "dp"), check_vma=False
    )
```

profile of v0, /device:TPU:24, one launch (start us, length us, event | category | flops | bytes accessed | tf_op | source)
XLA Modules:
  0.0 326.0 jit_solution(11963769279248139002)
XLA Ops:
  6.5 0.9 copy.44
  7.7 1.2 reduce-window.6
  9.4 0.7 fusion.38
  11.1 1.2 fusion.22
  12.4 2.2 fusion
  15.1 2.7 reduce.2
  17.8 2.2 reshape.192
  20.1 95.2 %all_to_all.10 = bf16[64,2,2048]{2,1,0:T(2,128)(2,1)} all-to-all(bf16[64,2,2048]{2,1,0:T(2,128)(2,1)} %reshape.192), channel_id=1, replica_groups=mesh['section'=2,'dp'=8,'expert'=64] {'expert'}, dimensions={0} | all-to-all | bytes 1048576 | tf_op jit(solution)/shard_map/all_to_all | solution.py:46
  115.3 4.5 %reshape.193 = bf16[64,1,4096]{2,1,0:T(2,128)(2,1)} reshape(bf16[64,2,2048]{2,1,0:T(2,128)(2,1)} %all_to_all.10) | data formatting | bytes 1048576
  119.7 2.6 copy.52
  122.4 31.4 %all-gather.6.cloned.1.call-done = bf16[64,8,4096]{2,0,1:T(8,128)(2,1)} async-done(((bf16[64,1,4096]{2,0,1:T(8,128)(2,1)}), bf16[64,8,4096]{2,0,1:T(8,128)(2,1)}) %all-gather.6.cloned.1.call-update) | async-done | bytes 4194320 | tf_op jit(solution)/shard_map/all_gather | solution.py:50
  153.9 4.5 %fusion.7 = f32[2,64,1,8,192]{4,1,0,3,2:T(8,128)S(1)} fusion(bf16[1,2,192,4096]{3,2,1,0:T(8,128)(2,1)S(1)} %copy-done, bf16[64,8,4096]{2,0,1:T(8,128)(2,1)} %all-gather.6.cloned.1.call-done), kind=kOutput, calls=%fused_computation.9 | convolution fusion | flops 1610612736 | bytes 8126464 | tf_op jit(solution)/shard_map/sekd,ejhd->jsekh/dot_general | solution.py:48
  158.6 1.0 copy.54
  159.5 45.9 %all-gather.4.cloned.1.call-done = bf16[64,1,8,1536]{0,2,1,3:T(8,128)(2,1)} async-done(((bf16[64,1,8,192]{0,2,1,3:T(8,128)(2,1)}), bf16[64,1,8,1536]{0,2,1,3:T(8,128)(2,1)}) %all-gather.4.cloned.1.call-update) | async-done | bytes 1572880 | tf_op jit(solution)/shard_map/all_gather | solution.py:57
  205.4 5.7 %copy.55 = bf16[64,1,8,1536]{3,2,0,1:T(8,128)(2,1)} copy(bf16[64,1,8,1536]{0,2,1,3:T(8,128)(2,1)} %all-gather.4.cloned.1.call-done) | data formatting | bytes 3145728 | tf_op jit(solution)/shard_map/all_gather | solution.py:57
  211.1 3.7 %fusion.17 = bf16[64,1,8,512]{3,2,1,0:T(8,128)(2,1)} fusion(bf16[1,1536,512]{2,1,0:T(8,128)(2,1)} %param.11, bf16[64,1,8,1536]{3,2,0,1:T(8,128)(2,1)} %copy.55), kind=kOutput, calls=%fused_computation.11 | convolution fusion | flops 805568512 | bytes 3670016 | tf_op jit(solution)/shard_map/sech,ehf->secf/dot_general | solution.py:55
  214.8 24.7 %all-to-all-start.1 = ((bf16[64,1,8,512]{3,2,1,0:T(8,128)(2,1)}), bf16[64,1,8,512]{3,2,1,0:T(8,128)(2,1)}, u32[]{:S(2)}, u32[]{:S(2)}) async-start(bf16[64,1,8,512]{3,2,1,0:T(8,128)(2,1)} %fusion.17), calls=%async_computation.1 | async-start | bytes 1048576 | tf_op jit(solution)/shard_map/all_to_all | solution.py:62
  239.5 2.1 convert_element_type.52
  242.1 62.6 %all-to-all-done.1 = bf16[64,1,8,512]{3,2,1,0:T(8,128)(2,1)} async-done(((bf16[64,1,8,512]{3,2,1,0:T(8,128)(2,1)}), bf16[64,1,8,512]{3,2,1,0:T(8,128)(2,1)}, u32[]{:S(2)}, u32[]{:S(2)}) %all-to-all-start.1) | async-done | bytes 524320 | tf_op jit(solution)/shard_map/all_to_all | solution.py:62
  304.6 3.8 %gather_fusion = bf16[512,512]{1,0:T(8,128)(2,1)} fusion(bf16[512,512]{1,0:T(8,128)(2,1)} %bitcast.23, s32[1024]{0:T(1024)S(1)} %pad_clamp_fusion), kind=kCustom, calls=%fused_computation | custom fusion | bytes 1050624 | tf_op jit(solution)/shard_map/jit(_take)/gather | solution.py:64
  308.4 1.5 multiply_reduce_fusion
  309.9 0.9 fusion.35
  310.8 3.3 %collective-permute-start = (bf16[64,512]{1,0:T(8,128)(2,1)S(1)}, bf16[64,512]{1,0:T(8,128)(2,1)S(1)}, u32[]{:S(2)}, u32[]{:S(2)}) collective-permute-start(bf16[64,512]{1,0:T(8,128)(2,1)S(1)} %fusion.35), channel_id=1, source_target_pairs={{512,0},{0,512},{513,1},{1,513},{514,2},{2,514},{515,3},{3,515},{5... | collective-permute-start | bytes 196616 | tf_op jit(solution)/shard_map/ppermute | solution.py:10
  314.2 4.3 %collective-permute-done = bf16[64,512]{1,0:T(8,128)(2,1)S(1)} collective-permute-done((bf16[64,512]{1,0:T(8,128)(2,1)S(1)}, bf16[64,512]{1,0:T(8,128)(2,1)S(1)}, u32[]{:S(2)}, u32[]{:S(2)}) %collective-permute-start) | collective-permute-done | bytes 65568 | tf_op jit(solution)/shard_map/ppermute | solution.py:10
  (34 shorter events, 3.5 us)
Async XLA Ops:
  6.5 147.3 %copy-start = (bf16[1,2,192,4096]{3,2,1,0:T(8,128)(2,1)S(1)}, bf16[1,2,192,4096]{3,2,1,0:T(8,128)(2,1)}, u32[]{:S(2)}) copy-start(bf16[1,2,192,4096]{3,2,1,0:T(8,128)(2,1)} %param.10) | copy-start | bytes 9437188
  6.5 147.3 %all-gather.6.cloned.1.call-start = ((), (), s32[]{:S(2)}) async-start(), calls=%async_computation.3 | async-start | bytes 4718592 | tf_op jit(solution)/shard_map/all_gather | solution.py:50
  122.4 83.1 %all-gather.4.cloned.1.call-start = ((), (), s32[]{:S(2)}) async-start(), calls=%async_computation.2 | async-start | bytes 3538944 | tf_op jit(solution)/shard_map/all_gather | solution.py:57
  211.1 30.6 %copy-start.1 = (s32[1,64,8]{1,2,0:T(8,128)S(1)}, s32[1,64,8]{1,2,0:T(8,128)}, u32[]{:S(2)}) copy-start(s32[1,64,8]{1,2,0:T(8,128)} %param.7) | copy-start | bytes 6148
  211.1 30.9 %copy-start.2 = (f32[1,64,8]{1,2,0:T(8,128)S(1)}, f32[1,64,8]{1,2,0:T(8,128)}, u32[]{:S(2)}) copy-start(f32[1,64,8]{1,2,0:T(8,128)} %param.8) | copy-start | bytes 6148
  214.8 89.8 %all-to-all-start.1 = ((bf16[64,1,8,512]{3,2,1,0:T(8,128)(2,1)}), bf16[64,1,8,512]{3,2,1,0:T(8,128)(2,1)}, u32[]{:S(2)}, u32[]{:S(2)}) async-start(bf16[64,1,8,512]{3,2,1,0:T(8,128)(2,1)} %fusion.17), calls=%async_computation.1 | async-start | bytes 1048576 | tf_op jit(solution)/shard_map/all_to_all | solution.py:62
  310.8 7.7 %collective-permute-start = (bf16[64,512]{1,0:T(8,128)(2,1)S(1)}, bf16[64,512]{1,0:T(8,128)(2,1)S(1)}, u32[]{:S(2)}, u32[]{:S(2)}) collective-permute-start(bf16[64,512]{1,0:T(8,128)(2,1)S(1)} %fusion.35), channel_id=1, source_target_pairs={{512,0},{0,512},{513,1},{1,513},{514,2},{2,514},{515,3},{3,515},{5... | collective-permute-start | bytes 196616 | tf_op jit(solution)/shard_map/ppermute | solution.py:10
Sparse Core Ops, SparseCore 0:
  122.5 31.3 all-gather.5
  159.7 45.7 all-gather.3
where the time goes:
time: 327 us; the launch traced here: 326 us
  waiting for transfers between devices  144 us (44%)
  blocking collectives  95.2 us (29%)
  starting transfers between devices  28.1 us (9%)
  local copies, waits for them, and re-layouts  22.8 us (7%)
  between operations  13.5 us (4%)
  other arithmetic  11.6 us (4%)
  matrix products  10.5 us (3%)
    all_to_all x1, blocking collectives, body(): lax.all_to_all(outgoing, 'expert', split_axis=0, concat_axis=0, tiled=True)  95.2 us
    all_to_all x1, waiting for transfers between devices, body(): lax.all_to_all(expert_out, 'expert', split_axis=0, concat_axis=0, tiled=T...  62.6 us
    all_gather x1, waiting for transfers between devices, body(): lax.all_gather(hidden_act, 'dp', axis=3, tiled=True)  45.9 us
    all_gather x1, waiting for transfers between devices, body(): lax.all_gather(arriving, 'dp', axis=2, tiled=True)  31.4 us
    all_to_all x1, starting transfers between devices, body(): lax.all_to_all(expert_out, 'expert', split_axis=0, concat_axis=0, tiled=T...  24.7 us
    unnamed x10, local copies, waits for them, and re-layouts  8.25 us
  transfers between devices with their start and end apart: 4, of which 4 were waited for; matrix products, arithmetic and copies ran while one was open for 1% of the time, Pallas kernels for 0%

commit v1 on v0

v1 whole, which is shorter than its diff:
```python
import functools

import jax
import jax.numpy as jnp
from jax import lax
from jax.experimental import pallas as pl
from jax.experimental.pallas import tpu as pltpu
from jax.sharding import PartitionSpec as P

MESH = pl.DeviceIdType.MESH
F32, BF16 = jnp.float32, jnp.bfloat16
CHUNKS = 4
GROUPS = 4


def remote(src, dst, send, recv, device):
    return pltpu.make_async_remote_copy(
        src_ref=src, dst_ref=dst, send_sem=send, recv_sem=recv, device_id=device, device_id_type=MESH
    )


def kernel(
    n_dp, n_exp,
    x_ref, rg_ref, gain_ref, gu_hbm, dn_hbm, out_ref,
    guv, dnv, blk, mt, cw, tri, ys, xg, ab, eo, rr, rbl, rbr, ct, oc, fin,
    load_sem, ring_s, ring_r, meta_s, meta_r, y_s, y_r, x_s, x_r, rel_s, rel_r, pc_s, pc_r,
    ax_s, ax_r, al_s, al_r, ap_s, ap_r, yb_s, yb_r, rs_s, rs_r, fin_s, fin_r,
):
    sec, dp, ex = lax.axis_index("section"), lax.axis_index("dp"), lax.axis_index("expert")
    n_z = n_exp // 2
    half = n_z // 2
    z, yl = ex // 2, lax.rem(ex, 2)
    tokens, width = blk.shape[1], blk.shape[2]
    part = tokens // CHUNKS
    right = (sec, dp, lax.rem(ex + 2, n_exp))
    left = (sec, dp, lax.rem(ex + n_exp - 2, n_exp))
    ynb = (sec, dp, ex + 1 - 2 * yl)
    dp_up, dp_down = lax.rem(dp + 2, n_dp), lax.rem(dp + n_dp - 2, n_dp)
    dp_far = lax.rem(dp + n_dp // 2, n_dp)
    dp_pc = dp + 1 - 2 * lax.rem(dp, 2)
    x_up, x_down, core = (sec, dp_up, ex), (sec, dp_down, ex), (sec, dp_pc, ex)
    over = (1 - sec, dp, ex)

    barrier = pltpu.get_barrier_semaphore()
    for peer in (right, left, ynb, x_up, x_down, core, over):
        pl.semaphore_signal(barrier, inc=1, device_id=peer, device_id_type=MESH)
    load_gu = pltpu.make_async_copy(gu_hbm, guv, load_sem.at[0])
    load_dn = pltpu.make_async_copy(dn_hbm, dnv, load_sem.at[1])
    load_gu.start()
    load_dn.start()

    wide = x_ref[...].astype(F32)
    scale = lax.rsqrt(jnp.mean(wide * wide, axis=-1, keepdims=True) + 1e-06)
    mine = pl.ds(pl.multiple_of(dp * width, width), width)
    blk[z] = (x_ref[:, mine].astype(F32) * scale * gain_ref[:, mine].astype(F32)).astype(BF16)
    mt[z] = rg_ref[...]
    a_tok = lax.broadcasted_iota(jnp.int32, (128, 128), 0)
    b_tok = lax.broadcasted_iota(jnp.int32, (128, 128), 1)
    tri[...] = jnp.where((a_tok < b_tok) & ((a_tok < 64) == (b_tok < 64)), 1.0, 0.0).astype(BF16)
    lane = lax.broadcasted_iota(jnp.int32, (8, 128), 1)
    sub = lax.broadcasted_iota(jnp.int32, (8, 128), 0)
    row16 = lax.broadcasted_iota(jnp.int32, (16, 128), 0).astype(F32)
    ex_own, ex_other = ex.astype(F32), (ex + 1 - 2 * yl).astype(F32)
    pl.semaphore_wait(barrier, 7)

    def ring(flow, k, piece):
        at = lax.rem(z + n_z - k, n_z) if flow == 0 else lax.rem(z + k, n_z)
        ref = blk.at[at, pl.ds(piece * part, part)]
        return ref, at

    def ring_send(flow, k, piece):
        ref, _ = ring(flow, k, piece)
        return remote(ref, ref, ring_s, ring_r.at[flow, k, piece], right if flow == 0 else left)

    def ring_wait(flow, k, piece):
        ref, _ = ring(flow, k, piece)
        remote(ref, ref, ring_s, ring_r.at[flow, k - 1, piece], right).wait_recv()

    def meta_send(flow, k):
        _, at = ring(flow, k, 0)
        return remote(mt.at[at], mt.at[at], meta_s, meta_r.at[flow, k], right if flow == 0 else left)

    def meta_wait(flow, k):
        _, at = ring(flow, k, 0)
        remote(mt.at[at], mt.at[at], meta_s, meta_r.at[flow, k - 1], right).wait_recv()

    def picks(p):
        code = cw[p]
        own = jnp.where(code[0:1] == row16, 1.0, 0.0)
        other = jnp.where(code[1:2] == row16, 1.0, 0.0)
        return code, own, other

    def choose(k, at_a, at_b):
        p = k - 1
        ma, mb = mt[at_a], mt[at_b]
        named = jnp.where(lane < 64, ma, pltpu.roll(mb, 64, 1))
        weight = jnp.where(lane < 64, pltpu.roll(ma, 64, 1), mb)
        hit_own, hit_other = named == ex_own, named == ex_other
        has_own = jnp.sum(jnp.where(hit_own, 1.0, 0.0), axis=0, keepdims=True)
        has_other = jnp.sum(jnp.where(hit_other, 1.0, 0.0), axis=0, keepdims=True)
        w_own = jnp.sum(jnp.where(hit_own, weight, 0.0), axis=0, keepdims=True)
        w_other = jnp.sum(jnp.where(hit_other, weight, 0.0), axis=0, keepdims=True)
        has = jnp.where(sub == 0, has_own, jnp.where(sub == 1, has_other, 0.0))
        rank = jnp.dot(has.astype(BF16), tri[...], preferred_element_type=F32)
        rank = jnp.where(lane < 64, rank, rank + 8.0)
        code = jnp.where(has > 0.5, rank, -100.0)
        cw[p] = jnp.where(sub < 2, code, jnp.where(sub == 2, w_own, w_other))
        own = jnp.where(code[0:1] == row16, 1.0, 0.0)
        other = jnp.where(code[1:2] == row16, 1.0, 0.0)
        pick = jnp.concatenate([own, other], axis=0).astype(BF16)
        both = jnp.concatenate([blk[at_a], blk[at_b]], axis=0)
        rows = jnp.dot(pick, both, preferred_element_type=F32).astype(BF16)
        xg[dp, p, 0:16, :] = rows[0:16]
        ys[p] = rows[16:32]
        remote(ys.at[p], xg.at[dp, p, 16:32], y_s, y_r.at[p], ynb).start()

    def spread(p):
        remote(ys.at[p], xg.at[dp, p, 16:32], y_s, y_r.at[p], ynb).wait_recv()
        here = xg.at[dp, p]
        remote(here, here, x_s, x_r.at[0, p], x_up).start()
        remote(here, here, x_s, x_r.at[1, p], x_down).start()
        remote(here, here, pc_s, pc_r.at[0, p], core).start()

    def relay(p):
        low, high = xg.at[dp_down, p], xg.at[dp_up, p]
        remote(low, low, x_s, x_r.at[0, p], x_up).wait_recv()
        first = xg.at[dp_down, p, 0:16]
        remote(first, first, rel_s, rel_r.at[0, p], x_up).start()
        remote(low, low, pc_s, pc_r.at[1, p], core).start()
        remote(high, high, x_s, x_r.at[1, p], x_up).wait_recv()
        second = xg.at[dp_up, p, 16:32]
        remote(second, second, rel_s, rel_r.at[1, p], x_down).start()
        remote(high, high, pc_s, pc_r.at[2, p], core).start()

    def hand_over(p):
        first, second = xg.at[dp_far, p, 0:16], xg.at[dp_far, p, 16:32]
        remote(first, first, rel_s, rel_r.at[0, p], x_up).wait_recv()
        remote(second, second, rel_s, rel_r.at[1, p], x_up).wait_recv()
        far = xg.at[dp_far, p]
        remote(far, far, pc_s, pc_r.at[3, p], core).start()

    def gathered(p):
        here = xg.at[dp, p]
        for i in range(4):
            remote(here, here, pc_s, pc_r.at[i, p], core).wait_recv()

    for piece in range(CHUNKS):
        ring_send(0, 0, piece).start()
        ring_send(1, 0, piece).start()
    meta_send(0, 0).start()
    meta_send(1, 0).start()

    def ring_step(k, more_a, take_b, more_b):
        for piece in range(CHUNKS):
            ring_wait(0, k, piece)
            if more_a:
                ring_send(0, k, piece).start()
            if take_b:
                ring_wait(1, k, piece)
            if more_b:
                ring_send(1, k, piece).start()
        meta_wait(0, k)
        if more_a:
            meta_send(0, k).start()
        if take_b:
            meta_wait(1, k)
        if more_b:
            meta_send(1, k).start()
        at_a = lax.rem(z + n_z - k, n_z)
        at_b = lax.rem(z + k, n_z) if take_b else z
        choose(k, at_a, at_b)

    def body(k, carry):
        ring_step(k, True, True, True)
        pl.when(k >= 2)(lambda: spread(k - 2))
        pl.when(k >= 3)(lambda: relay(k - 3))
        pl.when(k >= 4)(lambda: hand_over(k - 4))
        return carry

    lax.fori_loop(1, half - 1, body, 0)
    ring_step(half - 1, True, True, False)
    spread(half - 3)
    relay(half - 4)
    hand_over(half - 5)
    ring_step(half, False, False, False)
    spread(half - 2)
    relay(half - 3)
    hand_over(half - 4)
    spread(half - 1)
    relay(half - 2)
    hand_over(half - 3)
    relay(half - 1)
    hand_over(half - 2)
    hand_over(half - 1)
    lax.fori_loop(0, half, lambda p, c: (gathered(p), c)[1], 0)

    load_gu.wait()
    load_dn.wait()
    span = half // GROUPS
    rows = span * 32
    hidden = guv.shape[1]
    contract = (((1,), (1,)), ((), ()))

    def group_at(g):
        return (GROUPS - 1 - g) * span

    def expand(g):
        p0 = group_at(g)
        gate = up = None
        for d in range(n_dp):
            part_x = xg[d, p0:p0 + span].reshape(rows, width)
            cols = slice(d * width, (d + 1) * width)
            a = lax.dot_general(part_x, guv[0, :, cols], contract, preferred_element_type=F32)
            b = lax.dot_general(part_x, guv[1, :, cols], contract, preferred_element_type=F32)
            gate, up = (a, b) if gate is None else (gate + a, up + b)
        ab[dp, p0 * 32:p0 * 32 + rows, :] = (gate / (1.0 + jnp.exp(-gate)) * up).astype(BF16)
        here = ab.at[dp, p0 * 32:p0 * 32 + rows]
        remote(here, here, ax_s, ax_r.at[0, g], x_up).start()
        remote(here, here, ax_s, ax_r.at[1, g], x_down).start()
        remote(here, here, ap_s, ap_r.at[0, g], core).start()

    def act_relay(g):
        r0 = group_at(g) * 32
        mid, end = r0 + rows // 2, r0 + rows
        low, high = ab.at[dp_down, r0:end], ab.at[dp_up, r0:end]
        remote(low, low, ax_s, ax_r.at[0, g], x_up).wait_recv()
        first = ab.at[dp_down, r0:mid]
        remote(first, first, al_s, al_r.at[0, g], x_up).start()
        remote(low, low, ap_s, ap_r.at[1, g], core).start()
        remote(high, high, ax_s, ax_r.at[1, g], x_up).wait_recv()
        second = ab.at[dp_up, mid:end]
        remote(second, second, al_s, al_r.at[1, g], x_down).start()
        remote(high, high, ap_s, ap_r.at[2, g], core).start()

    def act_hand_over(g):
        r0 = group_at(g) * 32
        mid, end = r0 + rows // 2, r0 + rows
        first, second = ab.at[dp_far, r0:mid], ab.at[dp_far, mid:end]
        remote(first, first, al_s, al_r.at[0, g], x_up).wait_recv()
        remote(second, second, al_s, al_r.at[1, g], x_up).wait_recv()
        far = ab.at[dp_far, r0:end]
        remote(far, far, ap_s, ap_r.at[3, g], core).start()

    def contract_down(g):
        p0 = group_at(g)
        r0 = p0 * 32
        here = ab.at[dp, r0:r0 + rows]
        for i in range(4):
            remote(here, here, ap_s, ap_r.at[i, g], core).wait_recv()
        total = None
        for d in range(n_dp):
            a = jnp.dot(
                ab[d, r0:r0 + rows, :], dnv[d * hidden:(d + 1) * hidden, :], preferred_element_type=F32
            )
            total = a if total is None else total + a
        eo[p0:p0 + span] = total.astype(BF16).reshape(span, 32, width)
        rr[p0:p0 + span, 0:16, :] = eo[p0:p0 + span, 0:16, :]
        remote(
            eo.at[p0:p0 + span, 16:32], rr.at[p0:p0 + span, 16:32], yb_s, yb_r.at[g], ynb
        ).start()

    def swapped(g):
        p0 = group_at(g)
        there = rr.at[p0:p0 + span, 16:32]
        remote(there, there, yb_s, yb_r.at[g], ynb).wait_recv()

    expand(0)
    expand(1)
    act_relay(0)
    expand(2)
    act_hand_over(0)
    act_relay(1)
    contract_down(0)
    expand(3)
    act_hand_over(1)
    act_relay(2)
    contract_down(1)
    act_hand_over(2)
    act_relay(3)
    contract_down(2)
    act_hand_over(3)
    contract_down(3)
    for g in range(GROUPS):
        swapped(g)

    def share(k):
        code, own, other = picks(k - 1)
        w = jnp.concatenate([own * code[2:3], other * code[3:4]], axis=0)
        w_high = w.astype(BF16)
        w_low = (w - w_high.astype(F32)).astype(BF16)
        lhs = jnp.concatenate([w_high, w_low], axis=0)
        res = rr[k - 1]
        rhs = jnp.concatenate([res, res], axis=0)
        return lax.dot_general(lhs, rhs, (((0,), (0,)), ((), ())), preferred_element_type=F32)

    def back_send(flow, k, piece):
        buf = rbl if flow == 0 else rbr
        cut = pl.ds(piece * part, part)
        return remote(
            buf.at[k, cut], buf.at[k - 1, cut], rs_s, rs_r.at[flow, k - 1, piece], left if flow == 0 else right
        )

    def back_wait(flow, k, piece):
        buf = rbl if flow == 0 else rbr
        ref = buf.at[k, pl.ds(piece * part, part)]
        remote(ref, ref, rs_s, rs_r.at[flow, k, piece], left).wait_recv()

    def back_step(k, start_a, start_b):
        for piece in range(CHUNKS):
            lo = piece * part
            if not start_a:
                back_wait(0, k, piece)
            add = ct[lo:lo + part, :]
            if not start_a:
                add = add + rbl[k, lo:lo + part, :].astype(F32)
            rbl[k, lo:lo + part, :] = add.astype(BF16)
            back_send(0, k, piece).start()
            if start_b is None:
                continue
            if not start_b:
                back_wait(1, k, piece)
            add = ct[tokens + lo:tokens + lo + part, :]
            if not start_b:
                add = add + rbr[k, lo:lo + part, :].astype(F32)
            rbr[k, lo:lo + part, :] = add.astype(BF16)
            back_send(1, k, piece).start()

    ct[...] = share(half)
    oc[...] = ct[tokens:, :] + x_ref[:, mine].astype(F32)
    back_step(half, True, None)
    ct[...] = share(half - 1)
    back_step(half - 1, False, True)

    def back_body(i, carry):
        k = half - 2 - i
        ct[...] = share(k)
        back_step(k, False, False)
        return carry

    lax.fori_loop(0, half - 2, back_body, 0)
    for piece in range(CHUNKS):
        lo = piece * part
        back_wait(0, 0, piece)
        back_wait(1, 0, piece)
        fin[lo:lo + part, :] = (
            oc[lo:lo + part, :] + rbl[0, lo:lo + part, :].astype(F32) + rbr[0, lo:lo + part, :].astype(F32)
        ).astype(BF16)
    last = remote(fin, out_ref, fin_s, fin_r, over)
    last.start()

    def drained(ref, sem):
        remote(ref, ref, sem, sem, right).wait_send()

    drained(blk.at[0:n_z - 1], ring_s)
    drained(mt.at[0:n_z - 1], meta_s)
    drained(ys, y_s)
    drained(xg.at[0:2], x_s)
    drained(xg.at[0], rel_s)
    drained(xg.at[0:4], pc_s)
    drained(ab.at[0:2], ax_s)
    drained(ab.at[0], al_s)
    drained(ab.at[0:4], ap_s)
    drained(ys, yb_s)
    drained(blk.at[0:n_z - 1], rs_s)
    last.wait()


def body(activations, routes, gate_weights, norm_gain, gate_up_weights, down_weights):
    n_dp, n_exp = lax.axis_size("dp"), lax.axis_size("expert")
    tokens, features = activations.shape[1:]
    hidden = gate_up_weights.shape[2]
    width = features // n_dp
    n_z = n_exp // 2
    half = n_z // 2
    named = jnp.concatenate([routes[0].T.astype(F32), gate_weights[0].T], axis=1)
    vmem, anywhere = pl.BlockSpec(memory_space=pltpu.VMEM), pl.BlockSpec(memory_space=pl.ANY)
    dma = pltpu.SemaphoreType.DMA
    out = pl.pallas_call(
        functools.partial(kernel, n_dp, n_exp),
        out_shape=jax.ShapeDtypeStruct((tokens, width), BF16),
        in_specs=[vmem, vmem, vmem, anywhere, anywhere],
        out_specs=vmem,
        scratch_shapes=[
            pltpu.VMEM((2, hidden, features), BF16),
            pltpu.VMEM((hidden * n_dp, width), BF16),
            pltpu.VMEM((n_z, tokens, width), BF16),
            pltpu.VMEM((n_z, 8, 128), F32),
            pltpu.VMEM((half, 8, 128), F32),
            pltpu.VMEM((128, 128), BF16),
            pltpu.VMEM((half, 16, width), BF16),
            pltpu.VMEM((n_dp, half, 32, width), BF16),
            pltpu.VMEM((n_dp, half * 32, hidden), BF16),
            pltpu.VMEM((half, 32, width), BF16),
            pltpu.VMEM((half, 32, width), BF16),
            pltpu.VMEM((half + 1, tokens, width), BF16),
            pltpu.VMEM((half, tokens, width), BF16),
            pltpu.VMEM((2 * tokens, width), F32),
            pltpu.VMEM((tokens, width), F32),
            pltpu.VMEM((tokens, width), BF16),
            dma((2,)),
            dma, dma((2, half, CHUNKS)),
            dma, dma((2, half)),
            dma, dma((half,)),
            dma, dma((2, half)),
            dma, dma((2, half)),
            dma, dma((4, half)),
            dma, dma((2, GROUPS)),
            dma, dma((2, GROUPS)),
            dma, dma((4, GROUPS)),
            dma, dma((GROUPS,)),
            dma, dma((2, half, CHUNKS)),
            dma, dma,
        ],
        compiler_params=pltpu.CompilerParams(
            collective_id=0, has_side_effects=True, vmem_limit_bytes=56 * 1024 * 1024
        ),
    )(activations[0], named, norm_gain[None], gate_up_weights[0], down_weights[0])
    return out[None]


def solution(mesh):
    placed = (
        P("section", "expert", None),
        P("section", "expert", None),
        P("section", "expert", None),
        P(),
        P("expert", None, "dp", None),
        P("expert", None, "dp"),
    )
    return jax.shard_map(
        body, mesh=mesh, in_specs=placed, out_specs=P("section", "expert", "dp"), check_vma=False
    )
```

time: 327 us -> 172 us (0.53)
  the two profiles are of different devices: /device:TPU:24 before, /device:TPU:2 now
where the time goes in v1:
time: 172 us
  Pallas kernels  167 us (97%)
  local copies, waits for them, and re-layouts  2.78 us (2%)
  other arithmetic  2.04 us (1%)
    pallas_call x1, Pallas kernels, body(): pl.pallas_call(functools.partial(kernel, n_dp, n_exp), out_shape=jax.Shap...  167 us

profile of v1, /device:TPU:2, one launch (start us, length us, event | category | flops | bytes accessed | tf_op | source)
XLA Modules:
  0.0 172.1 jit_solution(8306002694001809232)
XLA Ops:
  0.0 0.7 convert_bitcast_fusion
  0.7 1.3 pad_maximum_fusion.rg_ref
  2.0 1.3 broadcast_in_dim.6.gain_ref
  3.4 167.2 %shard_map.64 = bf16[64,512]{1,0:T(8,128)(2,1)} custom-call(bf16[64,4096]{1,0:T(8,128)(2,1)} %bitcast.13, f32[8,128]{1,0:T(8,128)} %pad_maximum_fusion.rg_ref, bf16[1,4096]{1,0:T(2,128)(2,1)} %broadcast_in_dim.6.gain_ref, bf16[2,192,4096]{2,1,0:T(8,128)(2,1)} %bitcast.11, bf16[1536,512]{1,0:T(8,128)(2,1)} %bitcast.12), custom_call_target="tpu_custom_call" | custom-call | tf_op jit(solution)/shard_map/pallas_call | solution.py:378
  170.6 1.5 copy.8

commit v2 on v1

v2 whole, which is shorter than its diff:
```python
import functools

import jax
import jax.numpy as jnp
from jax import lax
from jax.experimental import pallas as pl
from jax.experimental.pallas import tpu as pltpu
from jax.sharding import PartitionSpec as P

MESH = pl.DeviceIdType.MESH
F32, BF16 = jnp.float32, jnp.bfloat16
CHUNKS = 2
GROUPS = 4


def remote(src, dst, send, recv, device):
    return pltpu.make_async_remote_copy(
        src_ref=src, dst_ref=dst, send_sem=send, recv_sem=recv, device_id=device, device_id_type=MESH
    )


def kernel(
    n_dp, n_exp,
    x_ref, routes_ref, gates_ref, gain_ref, gu_hbm, dn_hbm, out_ref,
    guv, dnv, blk, mt, cw, tri, ys, xg, ab, eo, rr, rbl, rbr, ct, oc, fin, lfl, lfr,
    load_sem, ring_s, ring_r, meta_s, meta_r, y_s, y_r, x_s, x_r, rel_s, rel_r, pc_s, pc_r,
    ax_s, ax_r, al_s, al_r, ap_s, ap_r, yb_s, yb_r, rs_s, rs_r, lf_s, lf_r, fin_s, fin_r,
):
    sec, dp, ex = lax.axis_index("section"), lax.axis_index("dp"), lax.axis_index("expert")
    n_z = n_exp // 2
    half = n_z // 2
    z, yl = ex // 2, lax.rem(ex, 2)
    tokens, width = blk.shape[1], blk.shape[2]
    part = tokens // CHUNKS
    right = (sec, dp, lax.rem(ex + 2, n_exp))
    left = (sec, dp, lax.rem(ex + n_exp - 2, n_exp))
    right2 = (sec, dp, lax.rem(ex + 4, n_exp))
    left2 = (sec, dp, lax.rem(ex + n_exp - 4, n_exp))
    ynb = (sec, dp, ex + 1 - 2 * yl)
    dp_up, dp_down = lax.rem(dp + 2, n_dp), lax.rem(dp + n_dp - 2, n_dp)
    dp_far = lax.rem(dp + n_dp // 2, n_dp)
    dp_pc = dp + 1 - 2 * lax.rem(dp, 2)
    x_up, x_down, core = (sec, dp_up, ex), (sec, dp_down, ex), (sec, dp_pc, ex)
    over = (1 - sec, dp, ex)

    barrier = pltpu.get_barrier_semaphore()
    for peer in (right, left, right2, left2, ynb, x_up, x_down, core, over):
        pl.semaphore_signal(barrier, inc=1, device_id=peer, device_id_type=MESH)
    load_gu = pltpu.make_async_copy(gu_hbm, guv, load_sem.at[0])
    load_dn = pltpu.make_async_copy(dn_hbm, dnv, load_sem.at[1])
    load_gu.start()
    load_dn.start()

    wide = x_ref[...].astype(F32)
    scale = lax.rsqrt(jnp.mean(wide * wide, axis=-1, keepdims=True) + 1e-06)
    mine = pl.ds(pl.multiple_of(dp * width, width), width)
    blk[z] = (x_ref[:, mine].astype(F32) * scale * gain_ref[:, mine].astype(F32)).astype(BF16)
    mt[z, :, 0:64] = routes_ref[...].astype(F32)
    mt[z, :, 64:128] = gates_ref[...]
    a_tok = lax.broadcasted_iota(jnp.int32, (128, 128), 0)
    b_tok = lax.broadcasted_iota(jnp.int32, (128, 128), 1)
    tri[...] = jnp.where((a_tok < b_tok) & ((a_tok < 64) == (b_tok < 64)), 1.0, 0.0).astype(BF16)
    lane = lax.broadcasted_iota(jnp.int32, (8, 128), 1)
    sub = lax.broadcasted_iota(jnp.int32, (8, 128), 0)
    row16 = lax.broadcasted_iota(jnp.int32, (16, 128), 0).astype(F32)
    ex_own, ex_other = ex.astype(F32), (ex + 1 - 2 * yl).astype(F32)
    pl.semaphore_wait(barrier, 9)

    def place(flow, k):
        return lax.rem(z + n_z - k, n_z) if flow == 0 else lax.rem(z + k, n_z)

    def target(flow, hops):
        return ((right, right2) if flow == 0 else (left, left2))[hops - 1]

    def ring_send(flow, k, hops, piece):
        ref = blk.at[place(flow, k), pl.ds(piece * part, part)]
        remote(ref, ref, ring_s, ring_r.at[flow, k + hops - 1, piece], target(flow, hops)).start()

    def ring_wait(flow, k, piece):
        ref = blk.at[place(flow, k), pl.ds(piece * part, part)]
        remote(ref, ref, ring_s, ring_r.at[flow, k - 1, piece], right).wait_recv()

    def meta_send(flow, k, hops):
        ref = mt.at[place(flow, k)]
        remote(ref, ref, meta_s, meta_r.at[flow, k + hops - 1], target(flow, hops)).start()

    def meta_wait(flow, k):
        ref = mt.at[place(flow, k)]
        remote(ref, ref, meta_s, meta_r.at[flow, k - 1], right).wait_recv()

    def picks(p):
        code = cw[p]
        own = jnp.where(code[0:1] == row16, 1.0, 0.0)
        other = jnp.where(code[1:2] == row16, 1.0, 0.0)
        return code, own, other

    def choose(k, at_a, at_b):
        p = k - 1
        ma, mb = mt[at_a], mt[at_b]
        named = jnp.where(lane < 64, ma, pltpu.roll(mb, 64, 1))
        weight = jnp.where(lane < 64, pltpu.roll(ma, 64, 1), mb)
        hit_own, hit_other = named == ex_own, named == ex_other
        has_own = jnp.sum(jnp.where(hit_own, 1.0, 0.0), axis=0, keepdims=True)
        has_other = jnp.sum(jnp.where(hit_other, 1.0, 0.0), axis=0, keepdims=True)
        w_own = jnp.sum(jnp.where(hit_own, weight, 0.0), axis=0, keepdims=True)
        w_other = jnp.sum(jnp.where(hit_other, weight, 0.0), axis=0, keepdims=True)
        has = jnp.where(sub == 0, has_own, jnp.where(sub == 1, has_other, 0.0))
        rank = jnp.dot(has.astype(BF16), tri[...], preferred_element_type=F32)
        rank = jnp.where(lane < 64, rank, rank + 8.0)
        code = jnp.where(has > 0.5, rank, -100.0)
        cw[p] = jnp.where(sub < 2, code, jnp.where(sub == 2, w_own, w_other))
        own = jnp.where(code[0:1] == row16, 1.0, 0.0)
        other = jnp.where(code[1:2] == row16, 1.0, 0.0)
        pick = jnp.concatenate([own, other], axis=0).astype(BF16)
        both = jnp.concatenate([blk[at_a], blk[at_b]], axis=0)
        rows = jnp.dot(pick, both, preferred_element_type=F32).astype(BF16)
        xg[dp, p, 0:16, :] = rows[0:16]
        ys[p] = rows[16:32]

    def swap(m):
        return remote(ys.at[pl.ds(2 * m, 2)], xg.at[dp, pl.ds(2 * m, 2), 16:32], y_s, y_r.at[m], ynb)

    def rows_of(d, m):
        return xg.at[d, pl.ds(2 * m, 2)]

    def spread(m):
        swap(m).wait_recv()
        here = rows_of(dp, m)
        remote(here, here, x_s, x_r.at[0, m], x_up).start()
        remote(here, here, x_s, x_r.at[1, m], x_down).start()
        remote(here, here, pc_s, pc_r.at[0, m], core).start()

    def relay(m):
        low, high = rows_of(dp_down, m), rows_of(dp_up, m)
        remote(low, low, x_s, x_r.at[0, m], x_up).wait_recv()
        first = xg.at[dp_down, 2 * m]
        remote(first, first, rel_s, rel_r.at[0, m], x_up).start()
        remote(high, high, x_s, x_r.at[1, m], x_up).wait_recv()
        second = xg.at[dp_up, 2 * m + 1]
        remote(second, second, rel_s, rel_r.at[1, m], x_down).start()
        remote(low, low, pc_s, pc_r.at[1, m], core).start()
        remote(high, high, pc_s, pc_r.at[2, m], core).start()

    def hand_over(m):
        first, second = xg.at[dp_far, 2 * m], xg.at[dp_far, 2 * m + 1]
        remote(first, first, rel_s, rel_r.at[0, m], x_up).wait_recv()
        remote(second, second, rel_s, rel_r.at[1, m], x_up).wait_recv()
        far = rows_of(dp_far, m)
        remote(far, far, pc_s, pc_r.at[3, m], core).start()

    def gathered(m):
        here = rows_of(dp, m)
        for i in range(4):
            remote(here, here, pc_s, pc_r.at[i, m], core).wait_recv()

    for piece in range(CHUNKS):
        for hops in (2, 1):
            for flow in (0, 1):
                ring_send(flow, 0, hops, piece)
    for hops in (2, 1):
        for flow in (0, 1):
            meta_send(flow, 0, hops)

    def ring_step(m, evens, sends):
        k = 2 * m
        for piece in range(CHUNKS):
            for flow in evens:
                ring_wait(flow, k, piece)
                for hops in sends[flow]:
                    ring_send(flow, k, hops, piece)
        for flow in evens:
            meta_wait(flow, k)
            for hops in sends[flow]:
                meta_send(flow, k, hops)
        for flow in (0, 1):
            for piece in range(CHUNKS):
                ring_wait(flow, k - 1, piece)
            meta_wait(flow, k - 1)
        choose(k - 1, place(0, k - 1), place(1, k - 1))
        choose(k, place(0, k), place(1, k) if 1 in evens else z)
        swap(m - 1).start()

    def body(m, carry):
        ring_step(m, (0, 1), ((2, 1), (2, 1)))
        pl.when(m >= 2)(lambda: spread(m - 2))
        pl.when(m >= 3)(lambda: relay(m - 3))
        pl.when(m >= 4)(lambda: hand_over(m - 4))
        return carry

    sets = half // 2
    lax.fori_loop(1, sets - 1, body, 0)
    ring_step(sets - 1, (0, 1), ((2, 1), (1,)))
    spread(sets - 3)
    relay(sets - 4)
    hand_over(sets - 5)
    ring_step(sets, (0,), ((), ()))
    spread(sets - 2)
    relay(sets - 3)
    hand_over(sets - 4)
    spread(sets - 1)
    relay(sets - 2)
    hand_over(sets - 3)
    relay(sets - 1)
    hand_over(sets - 2)
    hand_over(sets - 1)
    lax.fori_loop(0, sets, lambda m, c: (gathered(m), c)[1], 0)

    load_gu.wait()
    load_dn.wait()
    span = half // GROUPS
    rows = span * 32
    hidden = guv.shape[1]
    contract = (((1,), (1,)), ((), ()))

    def group_at(g):
        return (GROUPS - 1 - g) * span

    def expand(g):
        p0 = group_at(g)
        gate = up = None
        for d in range(n_dp):
            part_x = xg[d, p0:p0 + span].reshape(rows, width)
            cols = slice(d * width, (d + 1) * width)
            a = lax.dot_general(part_x, guv[0, :, cols], contract, preferred_element_type=F32)
            b = lax.dot_general(part_x, guv[1, :, cols], contract, preferred_element_type=F32)
            gate, up = (a, b) if gate is None else (gate + a, up + b)
        ab[dp, p0 * 32:p0 * 32 + rows, :] = (gate / (1.0 + jnp.exp(-gate)) * up).astype(BF16)
        here = ab.at[dp, p0 * 32:p0 * 32 + rows]
        remote(here, here, ax_s, ax_r.at[0, g], x_up).start()
        remote(here, here, ax_s, ax_r.at[1, g], x_down).start()
        remote(here, here, ap_s, ap_r.at[0, g], core).start()

    def act_relay(g):
        r0 = group_at(g) * 32
        mid, end = r0 + rows // 2, r0 + rows
        low, high = ab.at[dp_down, r0:end], ab.at[dp_up, r0:end]
        remote(low, low, ax_s, ax_r.at[0, g], x_up).wait_recv()
        first = ab.at[dp_down, r0:mid]
        remote(first, first, al_s, al_r.at[0, g], x_up).start()
        remote(low, low, ap_s, ap_r.at[1, g], core).start()
        remote(high, high, ax_s, ax_r.at[1, g], x_up).wait_recv()
        second = ab.at[dp_up, mid:end]
        remote(second, second, al_s, al_r.at[1, g], x_down).start()
        remote(high, high, ap_s, ap_r.at[2, g], core).start()

    def act_hand_over(g):
        r0 = group_at(g) * 32
        mid, end = r0 + rows // 2, r0 + rows
        first, second = ab.at[dp_far, r0:mid], ab.at[dp_far, mid:end]
        remote(first, first, al_s, al_r.at[0, g], x_up).wait_recv()
        remote(second, second, al_s, al_r.at[1, g], x_up).wait_recv()
        far = ab.at[dp_far, r0:end]
        remote(far, far, ap_s, ap_r.at[3, g], core).start()

    def contract_down(g):
        p0 = group_at(g)
        r0 = p0 * 32
        here = ab.at[dp, r0:r0 + rows]
        for i in range(4):
            remote(here, here, ap_s, ap_r.at[i, g], core).wait_recv()
        total = None
        for d in range(n_dp):
            a = jnp.dot(
                ab[d, r0:r0 + rows, :], dnv[d * hidden:(d + 1) * hidden, :], preferred_element_type=F32
            )
            total = a if total is None else total + a
        eo[p0:p0 + span] = total.astype(BF16).reshape(span, 32, width)
        rr[p0:p0 + span, 0:16, :] = eo[p0:p0 + span, 0:16, :]
        remote(
            eo.at[p0:p0 + span, 16:32], rr.at[p0:p0 + span, 16:32], yb_s, yb_r.at[g], ynb
        ).start()

    def swapped(g):
        p0 = group_at(g)
        there = rr.at[p0:p0 + span, 16:32]
        remote(there, there, yb_s, yb_r.at[g], ynb).wait_recv()

    def share(k):
        code, own, other = picks(k - 1)
        w = jnp.concatenate([own * code[2:3], other * code[3:4]], axis=0)
        w_high = w.astype(BF16)
        w_low = (w - w_high.astype(F32)).astype(BF16)
        lhs = jnp.concatenate([w_high, w_low], axis=0)
        res = rr[k - 1]
        rhs = jnp.concatenate([res, res], axis=0)
        return lax.dot_general(lhs, rhs, (((0,), (0,)), ((), ())), preferred_element_type=F32)

    def leaf_send(flow, k):
        buf = (lfl, lfr)[flow]
        half_ct = slice(0, tokens) if flow == 0 else slice(tokens, 2 * tokens)
        buf[k] = ct[1, half_ct, :].astype(BF16)
        remote(buf.at[k], buf.at[k - 1], lf_s, lf_r.at[flow, k - 1], target(1 - flow, 1)).start()

    def leaf_wait(flow, k):
        ref = (lfl, lfr)[flow].at[k]
        remote(ref, ref, lf_s, lf_r.at[flow, k], left).wait_recv()

    def back_wait(flow, k, piece):
        ref = (rbl, rbr)[flow].at[k, pl.ds(piece * part, part)]
        remote(ref, ref, rs_s, rs_r.at[flow, k, piece], left).wait_recv()

    def chain(flow, k, piece, leaf, more):
        buf, leaves = (rbl, rbr)[flow], (lfl, lfr)[flow]
        cut = slice(piece * part, (piece + 1) * part)
        add = ct[0, flow * tokens + piece * part:flow * tokens + (piece + 1) * part, :]
        if leaf:
            add = add + leaves[k, cut, :].astype(F32)
        if more:
            back_wait(flow, k, piece)
            add = add + buf[k, cut, :].astype(F32)
        buf[k, cut, :] = add.astype(BF16)
        remote(
            buf.at[k, cut], buf.at[k - 2, cut], rs_s, rs_r.at[flow, k - 2, piece], target(1 - flow, 2)
        ).start()

    def shares_for(m):
        ct[0] = share(2 * m)
        ct[1] = share(2 * m - 1)

    def back_step(m):
        k = 2 * m
        if k < half:
            leaf_wait(0, k)
            leaf_wait(1, k)
        for piece in range(CHUNKS):
            chain(0, k, piece, k < half, k < half)
            if k < half:
                chain(1, k, piece, True, k < half - 2)
        leaf_send(0, k - 1)
        leaf_send(1, k - 1)

    def back_pair(g):
        m = (GROUPS - g) * span // 2
        swapped(g)
        shares_for(m)
        if g == 0:
            oc[...] = ct[0, tokens:, :] + x_ref[:, mine].astype(F32)
        back_step(m)
        shares_for(m - 1)
        return m - 1

    expand(0)
    expand(1)
    act_relay(0)
    expand(2)
    act_hand_over(0)
    act_relay(1)
    contract_down(0)
    expand(3)
    act_hand_over(1)
    m = back_pair(0)
    act_relay(2)
    contract_down(1)
    back_step(m)
    m = back_pair(1)
    act_hand_over(2)
    act_relay(3)
    contract_down(2)
    back_step(m)
    m = back_pair(2)
    act_hand_over(3)
    contract_down(3)
    back_step(m)
    m = back_pair(3)
    back_step(m)
    leaf_wait(0, 0)
    leaf_wait(1, 0)
    for piece in range(CHUNKS):
        cut = slice(piece * part, (piece + 1) * part)
        near = oc[cut, :] + lfl[0, cut, :].astype(F32) + lfr[0, cut, :].astype(F32)
        back_wait(0, 0, piece)
        back_wait(1, 0, piece)
        fin[cut, :] = (near + rbl[0, cut, :].astype(F32) + rbr[0, cut, :].astype(F32)).astype(BF16)
    last = remote(fin, out_ref, fin_s, fin_r, over)
    last.start()

    def drained(ref, sem):
        remote(ref, ref, sem, sem, right).wait_send()

    drained(blk.at[0:n_z - 1], ring_s)
    drained(mt.at[0:n_z - 1], meta_s)
    drained(ys, y_s)
    drained(xg.at[0:2], x_s)
    drained(xg.at[0], rel_s)
    drained(xg.at[0:4], pc_s)
    drained(ab.at[0:2], ax_s)
    drained(ab.at[0], al_s)
    drained(ab.at[0:4], ap_s)
    drained(ys, yb_s)
    drained(blk.at[0:half - 1], rs_s)
    drained(blk.at[0:half], lf_s)
    last.wait()


def body(activations, routes, gate_weights, norm_gain, gate_up_weights, down_weights):
    n_dp, n_exp = lax.axis_size("dp"), lax.axis_size("expert")
    tokens, features = activations.shape[1:]
    hidden = gate_up_weights.shape[2]
    width = features // n_dp
    n_z = n_exp // 2
    half = n_z // 2
    vmem, anywhere = pl.BlockSpec(memory_space=pltpu.VMEM), pl.BlockSpec(memory_space=pl.ANY)
    dma = pltpu.SemaphoreType.DMA
    out = pl.pallas_call(
        functools.partial(kernel, n_dp, n_exp),
        out_shape=jax.ShapeDtypeStruct((tokens, width), BF16),
        in_specs=[vmem, vmem, vmem, vmem, anywhere, anywhere],
        out_specs=vmem,
        scratch_shapes=[
            pltpu.VMEM((2, hidden, features), BF16),
            pltpu.VMEM((hidden * n_dp, width), BF16),
            pltpu.VMEM((n_z, tokens, width), BF16),
            pltpu.VMEM((n_z, 8, 128), F32),
            pltpu.VMEM((half, 8, 128), F32),
            pltpu.VMEM((128, 128), BF16),
            pltpu.VMEM((half, 16, width), BF16),
            pltpu.VMEM((n_dp, half, 32, width), BF16),
            pltpu.VMEM((n_dp, half * 32, hidden), BF16),
            pltpu.VMEM((half, 32, width), BF16),
            pltpu.VMEM((half, 32, width), BF16),
            pltpu.VMEM((half + 1, tokens, width), BF16),
            pltpu.VMEM((half, tokens, width), BF16),
            pltpu.VMEM((2, 2 * tokens, width), F32),
            pltpu.VMEM((tokens, width), F32),
            pltpu.VMEM((tokens, width), BF16),
            pltpu.VMEM((half, tokens, width), BF16),
            pltpu.VMEM((half, tokens, width), BF16),
            dma((2,)),
            dma, dma((2, half, CHUNKS)),
            dma, dma((2, half)),
            dma, dma((half // 2,)),
            dma, dma((2, half // 2)),
            dma, dma((2, half // 2)),
            dma, dma((4, half // 2)),
            dma, dma((2, GROUPS)),
            dma, dma((2, GROUPS)),
            dma, dma((4, GROUPS)),
            dma, dma((GROUPS,)),
            dma, dma((2, half, CHUNKS)),
            dma, dma((2, half)),
            dma, dma,
        ],
        compiler_params=pltpu.CompilerParams(
            collective_id=0, has_side_effects=True, vmem_limit_bytes=56 * 1024 * 1024
        ),
    )(activations[0], routes[0].T, gate_weights[0].T, norm_gain[None], gate_up_weights[0], down_weights[0])
    return out[None]


def solution(mesh):
    placed = (
        P("section", "expert", None),
        P("section", "expert", None),
        P("section", "expert", None),
        P(),
        P("expert", None, "dp", None),
        P("expert", None, "dp"),
    )
    return jax.shard_map(
        body, mesh=mesh, in_specs=placed, out_specs=P("section", "expert", "dp"), check_vma=False
    )
```

time: 172 us -> 144 us (0.84)
  Pallas kernels: 167 us -> 141 us
  other arithmetic: 2.04 us -> 0 us
    pallas_call x1, Pallas kernels: 167 us -> 141 us  [body(): pl.pallas_call(functools.partial(kernel, n_dp, n_exp), out_shape=jax.Shap...]
where the time goes in v2:
time: 144 us
  Pallas kernels  141 us (98%)
  local copies, waits for them, and re-layouts  2.78 us (2%)
    pallas_call x1, Pallas kernels, body(): pl.pallas_call(functools.partial(kernel, n_dp, n_exp), out_shape=jax.Shap...  141 us

profile of v2, /device:TPU:2, one launch (start us, length us, event | category | flops | bytes accessed | tf_op | source)
XLA Modules:
  0.0 143.9 jit_solution(13793801123150268830)
XLA Ops:
  0.0 1.3 broadcast_in_dim.6.gain_ref
  1.3 141.1 %shard_map.64 = bf16[64,512]{1,0:T(8,128)(2,1)} custom-call(bf16[64,4096]{1,0:T(8,128)(2,1)} %bitcast.12, s32[8,64]{1,0:T(8,128)} %bitcast.14, f32[8,64]{1,0:T(8,128)} %bitcast.15, bf16[1,4096]{1,0:T(2,128)(2,1)} %broadcast_in_dim.6.gain_ref, bf16[2,192,4096]{2,1,0:T(8,128)(2,1)} %bitcast.10, bf16[1536,512]{1,0:T(8,128)(2,1)} %bitcast.11), custom_call_target="tpu_custom_call" | custom-call | tf_op jit(solution)/shard_map/pallas_call | solution.py:404
  142.4 1.5 %copy.8 = bf16[1,64,512]{2,1,0:T(8,128)(2,1)} copy(bf16[1,64,512]{2,1,0:T(8,128)(2,1)} %bitcast.13) | data formatting | bytes 131072

commit v3 on v2

--- a/solution.py
+++ b/solution.py
@@ -22,8 +22,8 @@
 def kernel(
     n_dp, n_exp,
     x_ref, routes_ref, gates_ref, gain_ref, gu_hbm, dn_hbm, out_ref,
-    guv, dnv, blk, mt, cw, tri, ys, xg, ab, eo, rr, rbl, rbr, ct, oc, fin, lfl, lfr,
-    load_sem, ring_s, ring_r, meta_s, meta_r, y_s, y_r, x_s, x_r, rel_s, rel_r, pc_s, pc_r,
+    guv, dnv, blk, mt, cw, tri, ys, xg, ab, eo, rr, rbl, rbr, ct, oc, fin, lin, lout, bin_, bout,
+    load_sem, ring_s, ring_r, meta_s, meta_r, leaf_s, leaf_r, y_s, y_r, x_s, x_r, rel_s, rel_r, pc_s, pc_r,
     ax_s, ax_r, al_s, al_r, ap_s, ap_r, yb_s, yb_r, rs_s, rs_r, lf_s, lf_r, fin_s, fin_r,
 ):
     sec, dp, ex = lax.axis_index("section"), lax.axis_index("dp"), lax.axis_index("expert")
@@ -63,7 +63,16 @@
     lane = lax.broadcasted_iota(jnp.int32, (8, 128), 1)
     sub = lax.broadcasted_iota(jnp.int32, (8, 128), 0)
     row16 = lax.broadcasted_iota(jnp.int32, (16, 128), 0).astype(F32)
-    ex_own, ex_other = ex.astype(F32), (ex + 1 - 2 * yl).astype(F32)
+    low16 = lax.broadcasted_iota(jnp.int32, (16, 128), 1) < 64
+    first16 = row16 < 8.0
+    mate = 1 - 2 * yl
+    ahead, behind = lax.rem(ex + 2, n_exp), lax.rem(ex + n_exp - 2, n_exp)
+    wanted = (
+        jnp.full((8, 128), ex, jnp.int32),
+        jnp.full((8, 128), ex + mate, jnp.int32),
+        jnp.where(lane < 64, ahead, behind),
+        jnp.where(lane < 64, ahead + mate, behind + mate),
+    )
     pl.semaphore_wait(barrier, 9)
 
     def place(flow, k):
@@ -72,50 +81,64 @@
     def target(flow, hops):
         return ((right, right2) if flow == 0 else (left, left2))[hops - 1]
 
-    def ring_send(flow, k, hops, piece):
-        ref = blk.at[place(flow, k), pl.ds(piece * part, part)]
-        remote(ref, ref, ring_s, ring_r.at[flow, k + hops - 1, piece], target(flow, hops)).start()
-
-    def ring_wait(flow, k, piece):
-        ref = blk.at[place(flow, k), pl.ds(piece * part, part)]
-        remote(ref, ref, ring_s, ring_r.at[flow, k - 1, piece], right).wait_recv()
-
-    def meta_send(flow, k, hops):
-        ref = mt.at[place(flow, k)]
-        remote(ref, ref, meta_s, meta_r.at[flow, k + hops - 1], target(flow, hops)).start()
-
-    def meta_wait(flow, k):
-        ref = mt.at[place(flow, k)]
-        remote(ref, ref, meta_s, meta_r.at[flow, k - 1], right).wait_recv()
-
-    def picks(p):
-        code = cw[p]
+    def ring_send(flow, j, piece):
+        ref = blk.at[place(flow, 2 * j), pl.ds(piece * part, part)]
+        remote(ref, ref, ring_s, ring_r.at[flow, j, piece], target(flow, 2)).start()
+
+    def ring_wait(flow, j, piece):
+        ref = blk.at[place(flow, 2 * j), pl.ds(piece * part, part)]
+        remote(ref, ref, ring_s, ring_r.at[flow, j - 1, piece], right).wait_recv()
+
+    def meta_send(flow, j):
+        ref = mt.at[place(flow, 2 * j)]
+        remote(ref, ref, meta_s, meta_r.at[flow, j], target(flow, 2)).start()
+
+    def meta_wait(flow, j):
+        ref = mt.at[place(flow, 2 * j)]
+        remote(ref, ref, meta_s, meta_r.at[flow, j - 1], right).wait_recv()
+
+    def masks(code):
         own = jnp.where(code[0:1] == row16, 1.0, 0.0)
         other = jnp.where(code[1:2] == row16, 1.0, 0.0)
-        return code, own, other
-
-    def choose(k, at_a, at_b):
-        p = k - 1
+        at_a = jnp.where(first16, code[2:3], code[3:4] + 8.0)
+        at_b = jnp.where(first16, code[2:3] - 8.0, code[3:4])
+        leaf_a = jnp.where((at_a == row16) & low16, 1.0, 0.0)
+        leaf_b = jnp.where((at_b == row16) & ~low16, 1.0, 0.0)
+        return own, other, leaf_a, leaf_b
+
+    def choose(j, at_a, at_b, own, leaf):
         ma, mb = mt[at_a], mt[at_b]
         named = jnp.where(lane < 64, ma, pltpu.roll(mb, 64, 1))
         weight = jnp.where(lane < 64, pltpu.roll(ma, 64, 1), mb)
-        hit_own, hit_other = named == ex_own, named == ex_other
-        has_own = jnp.sum(jnp.where(hit_own, 1.0, 0.0), axis=0, keepdims=True)
-        has_other = jnp.sum(jnp.where(hit_other, 1.0, 0.0), axis=0, keepdims=True)
-        w_own = jnp.sum(jnp.where(hit_own, weight, 0.0), axis=0, keepdims=True)
-        w_other = jnp.sum(jnp.where(hit_other, weight, 0.0), axis=0, keepdims=True)
-        has = jnp.where(sub == 0, has_own, jnp.where(sub == 1, has_other, 0.0))
+        has = weights = jnp.zeros((8, 128), F32)
+        for i, expert in enumerate(wanted):
+            hit = named == expert.astype(F32)
+            has = jnp.where(sub == i, jnp.sum(jnp.where(hit, 1.0, 0.0), axis=0, keepdims=True), has)
+            weights = jnp.where(sub == 4 + i, jnp.sum(jnp.where(hit, weight, 0.0), axis=0, keepdims=True), weights)
         rank = jnp.dot(has.astype(BF16), tri[...], preferred_element_type=F32)
         rank = jnp.where(lane < 64, rank, rank + 8.0)
-        code = jnp.where(has > 0.5, rank, -100.0)
-        cw[p] = jnp.where(sub < 2, code, jnp.where(sub == 2, w_own, w_other))
-        own = jnp.where(code[0:1] == row16, 1.0, 0.0)
-        other = jnp.where(code[1:2] == row16, 1.0, 0.0)
-        pick = jnp.concatenate([own, other], axis=0).astype(BF16)
+        code = jnp.where(sub < 4, jnp.where(has > 0.5, rank, -100.0), weights)
+        cw[j] = code
+        mask = masks(code)
+        mask = (mask[:2] if own else ()) + (mask[2:] if leaf else ())
+        pick = jnp.concatenate(mask, axis=0).astype(BF16)
         both = jnp.concatenate([blk[at_a], blk[at_b]], axis=0)
         rows = jnp.dot(pick, both, preferred_element_type=F32).astype(BF16)
-        xg[dp, p, 0:16, :] = rows[0:16]
-        ys[p] = rows[16:32]
+        if leaf:
+            lout[0, j] = rows[-32:-16]
+            lout[1, j] = rows[-16:]
+            for flow in (0, 1):
+                remote(lout.at[flow, j], lin.at[flow, j], leaf_s, leaf_r.at[flow, j], target(flow, 1)).start()
+        if own:
+            xg[dp, 2 * j - 1, 0:16, :] = rows[0:16]
+            ys[2 * j - 1] = rows[16:32]
+
+    def take_leaf(j):
+        for flow in (0, 1):
+            remote(lin.at[flow, j], lin.at[flow, j], leaf_s, leaf_r.at[flow, j], right).wait_recv()
+        a, b = lin[0, j].astype(F32), lin[1, j].astype(F32)
+        xg[dp, 2 * j, 0:16, :] = jnp.concatenate([a[0:8], b[0:8]], axis=0).astype(BF16)
+        ys[2 * j] = jnp.concatenate([a[8:16], b[8:16]], axis=0).astype(BF16)
 
     def swap(m):
         return remote(ys.at[pl.ds(2 * m, 2)], xg.at[dp, pl.ds(2 * m, 2), 16:32], y_s, y_r.at[m], ynb)
@@ -154,34 +177,29 @@
             remote(here, here, pc_s, pc_r.at[i, m], core).wait_recv()
 
     for piece in range(CHUNKS):
-        for hops in (2, 1):
-            for flow in (0, 1):
-                ring_send(flow, 0, hops, piece)
-    for hops in (2, 1):
         for flow in (0, 1):
-            meta_send(flow, 0, hops)
+            ring_send(flow, 0, piece)
+    for flow in (0, 1):
+        meta_send(flow, 0)
+    choose(0, z, z, False, True)
 
     def ring_step(m, evens, sends):
-        k = 2 * m
         for piece in range(CHUNKS):
             for flow in evens:
-                ring_wait(flow, k, piece)
-                for hops in sends[flow]:
-                    ring_send(flow, k, hops, piece)
+                ring_wait(flow, m, piece)
+                if flow in sends:
+                    ring_send(flow, m, piece)
         for flow in evens:
-            meta_wait(flow, k)
-            for hops in sends[flow]:
-                meta_send(flow, k, hops)
-        for flow in (0, 1):
-            for piece in range(CHUNKS):
-                ring_wait(flow, k - 1, piece)
-            meta_wait(flow, k - 1)
-        choose(k - 1, place(0, k - 1), place(1, k - 1))
-        choose(k, place(0, k), place(1, k) if 1 in evens else z)
+            meta_wait(flow, m)
+            if flow in sends:
+                meta_send(flow, m)
+        last = len(evens) == 1
+        choose(m, place(0, 2 * m), z if last else place(1, 2 * m), True, not last)
+        take_leaf(m - 1)
         swap(m - 1).start()
 
     def body(m, carry):
-        ring_step(m, (0, 1), ((2, 1), (2, 1)))
+        ring_step(m, (0, 1), (0, 1))
         pl.when(m >= 2)(lambda: spread(m - 2))
         pl.when(m >= 3)(lambda: relay(m - 3))
         pl.when(m >= 4)(lambda: hand_over(m - 4))
@@ -189,21 +207,10 @@
 
     sets = half // 2
     lax.fori_loop(1, sets - 1, body, 0)
-    ring_step(sets - 1, (0, 1), ((2, 1), (1,)))
+    ring_step(sets - 1, (0, 1), (0,))
     spread(sets - 3)
     relay(sets - 4)
     hand_over(sets - 5)
-    ring_step(sets, (0,), ((), ()))
-    spread(sets - 2)
-    relay(sets - 3)
-    hand_over(sets - 4)
-    spread(sets - 1)
-    relay(sets - 2)
-    hand_over(sets - 3)
-    relay(sets - 1)
-    hand_over(sets - 2)
-    hand_over(sets - 1)
-    lax.fori_loop(0, sets, lambda m, c: (gathered(m), c)[1], 0)
 
     load_gu.wait()
     load_dn.wait()
@@ -275,110 +282,123 @@
         there = rr.at[p0:p0 + span, 16:32]
         remote(there, there, yb_s, yb_r.at[g], ynb).wait_recv()
 
-    def share(k):
-        code, own, other = picks(k - 1)
-        w = jnp.concatenate([own * code[2:3], other * code[3:4]], axis=0)
+    def leaves_send(g):
+        for p in range(group_at(g), group_at(g) + span, 2):
+            j = p // 2
+            res = rr[p].astype(F32)
+            bout[0, j] = jnp.concatenate([res[0:8], res[16:24]], axis=0).astype(BF16)
+            bout[1, j] = jnp.concatenate([res[8:16], res[24:32]], axis=0).astype(BF16)
+            for flow in (0, 1):
+                remote(
+                    bout.at[flow, j], bin_.at[flow, j], lf_s, lf_r.at[flow, j], target(1 - flow, 1)
+                ).start()
+
+    def share(j, own, leaf):
+        code = cw[j]
+        own_m, other_m, leaf_a, leaf_b = masks(code)
+        w, res = (), ()
+        if own:
+            w += (own_m * code[4:5], other_m * code[5:6])
+            res += (rr[2 * j - 1],)
+        if leaf:
+            for flow in (0, 1):
+                remote(bin_.at[flow, j], bin_.at[flow, j], lf_s, lf_r.at[flow, j], left).wait_recv()
+            by = jnp.where(first16, code[6:7], code[7:8])
+            w += (leaf_a * by, leaf_b * by)
+            res += (bin_[0, j], bin_[1, j])
+        w = jnp.concatenate(w, axis=0)
         w_high = w.astype(BF16)
         w_low = (w - w_high.astype(F32)).astype(BF16)
         lhs = jnp.concatenate([w_high, w_low], axis=0)
-        res = rr[k - 1]
-        rhs = jnp.concatenate([res, res], axis=0)
+        rhs = jnp.concatenate(res + res, axis=0)
         return lax.dot_general(lhs, rhs, (((0,), (0,)), ((), ())), preferred_element_type=F32)
 
-    def leaf_send(flow, k):
-        buf = (lfl, lfr)[flow]
-        half_ct = slice(0, tokens) if flow == 0 else slice(tokens, 2 * tokens)
-        buf[k] = ct[1, half_ct, :].astype(BF16)
-        remote(buf.at[k], buf.at[k - 1], lf_s, lf_r.at[flow, k - 1], target(1 - flow, 1)).start()
-
-    def leaf_wait(flow, k):
-        ref = (lfl, lfr)[flow].at[k]
-        remote(ref, ref, lf_s, lf_r.at[flow, k], left).wait_recv()
-
-    def back_wait(flow, k, piece):
-        ref = (rbl, rbr)[flow].at[k, pl.ds(piece * part, part)]
-        remote(ref, ref, rs_s, rs_r.at[flow, k, piece], left).wait_recv()
-
-    def chain(flow, k, piece, leaf, more):
-        buf, leaves = (rbl, rbr)[flow], (lfl, lfr)[flow]
+    def back_wait(flow, j, piece):
+        ref = (rbl, rbr)[flow].at[j, pl.ds(piece * part, part)]
+        remote(ref, ref, rs_s, rs_r.at[flow, j, piece], left).wait_recv()
+
+    def chain(flow, j, piece, more):
+        buf = (rbl, rbr)[flow]
         cut = slice(piece * part, (piece + 1) * part)
-        add = ct[0, flow * tokens + piece * part:flow * tokens + (piece + 1) * part, :]
-        if leaf:
-            add = add + leaves[k, cut, :].astype(F32)
+        add = ct[flow * tokens + piece * part:flow * tokens + (piece + 1) * part, :]
         if more:
-            back_wait(flow, k, piece)
-            add = add + buf[k, cut, :].astype(F32)
-        buf[k, cut, :] = add.astype(BF16)
+            back_wait(flow, j, piece)
+            add = add + buf[j, cut, :].astype(F32)
+        buf[j, cut, :] = add.astype(BF16)
         remote(
-            buf.at[k, cut], buf.at[k - 2, cut], rs_s, rs_r.at[flow, k - 2, piece], target(1 - flow, 2)
+            buf.at[j, cut], buf.at[j - 1, cut], rs_s, rs_r.at[flow, j - 1, piece], target(1 - flow, 2)
         ).start()
 
-    def shares_for(m):
-        ct[0] = share(2 * m)
-        ct[1] = share(2 * m - 1)
-
-    def back_step(m):
-        k = 2 * m
-        if k < half:
-            leaf_wait(0, k)
-            leaf_wait(1, k)
+    def back_step(j):
         for piece in range(CHUNKS):
-            chain(0, k, piece, k < half, k < half)
-            if k < half:
-                chain(1, k, piece, True, k < half - 2)
-        leaf_send(0, k - 1)
-        leaf_send(1, k - 1)
+            chain(0, j, piece, j < sets)
+            if j < sets:
+                chain(1, j, piece, j < sets - 1)
 
     def back_pair(g):
-        m = (GROUPS - g) * span // 2
+        j = (GROUPS - g) * span // 2
         swapped(g)
-        shares_for(m)
+        leaves_send(g)
+        ct[...] = share(j, True, g > 0)
         if g == 0:
-            oc[...] = ct[0, tokens:, :] + x_ref[:, mine].astype(F32)
-        back_step(m)
-        shares_for(m - 1)
-        return m - 1
-
+            oc[...] = ct[tokens:, :] + x_ref[:, mine].astype(F32)
+        back_step(j)
+        ct[...] = share(j - 1, True, True)
+        return j - 1
+
+    ring_step(sets, (0,), ())
+    spread(sets - 2)
+    relay(sets - 3)
+    hand_over(sets - 4)
+    gathered(0)
+    gathered(1)
+    expand(3)
+    spread(sets - 1)
+    relay(sets - 2)
+    hand_over(sets - 3)
+    gathered(2)
+    gathered(3)
+    expand(2)
+    relay(sets - 1)
+    hand_over(sets - 2)
+    act_relay(3)
+    gathered(4)
+    gathered(5)
+    expand(1)
+    hand_over(sets - 1)
+    act_hand_over(3)
+    act_relay(2)
+    gathered(6)
+    gathered(7)
     expand(0)
-    expand(1)
+    act_relay(1)
+    act_hand_over(2)
+    contract_down(3)
     act_relay(0)
-    expand(2)
+    act_hand_over(1)
+    contract_down(2)
     act_hand_over(0)
-    act_relay(1)
+    contract_down(1)
     contract_down(0)
-    expand(3)
-    act_hand_over(1)
-    m = back_pair(0)
-    act_relay(2)
-    contract_down(1)
-    back_step(m)
-    m = back_pair(1)
-    act_hand_over(2)
-    act_relay(3)
-    contract_down(2)
-    back_step(m)
-    m = back_pair(2)
-    act_hand_over(3)
-    contract_down(3)
-    back_step(m)
-    m = back_pair(3)
-    back_step(m)
-    leaf_wait(0, 0)
-    leaf_wait(1, 0)
+    for g in range(GROUPS):
+        j = back_pair(g)
+        back_step(j)
+    ct[...] = share(0, False, True)
+    oc[...] = oc[...] + ct[0:tokens, :] + ct[tokens:, :]
     for piece in range(CHUNKS):
         cut = slice(piece * part, (piece + 1) * part)
-        near = oc[cut, :] + lfl[0, cut, :].astype(F32) + lfr[0, cut, :].astype(F32)
         back_wait(0, 0, piece)
         back_wait(1, 0, piece)
-        fin[cut, :] = (near + rbl[0, cut, :].astype(F32) + rbr[0, cut, :].astype(F32)).astype(BF16)
+        fin[cut, :] = (oc[cut, :] + rbl[0, cut, :].astype(F32) + rbr[0, cut, :].astype(F32)).astype(BF16)
     last = remote(fin, out_ref, fin_s, fin_r, over)
     last.start()
 
     def drained(ref, sem):
         remote(ref, ref, sem, sem, right).wait_send()
 
-    drained(blk.at[0:n_z - 1], ring_s)
-    drained(mt.at[0:n_z - 1], meta_s)
+    drained(blk.at[0:half - 1], ring_s)
+    drained(mt.at[0:half - 1], meta_s)
+    drained(lout, leaf_s)
     drained(ys, y_s)
     drained(xg.at[0:2], x_s)
     drained(xg.at[0], rel_s)
@@ -388,7 +408,7 @@
     drained(ab.at[0:4], ap_s)
     drained(ys, yb_s)
     drained(blk.at[0:half - 1], rs_s)
-    drained(blk.at[0:half], lf_s)
+    drained(bout, lf_s)
     last.wait()
 
 
@@ -411,23 +431,26 @@
             pltpu.VMEM((hidden * n_dp, width), BF16),
             pltpu.VMEM((n_z, tokens, width), BF16),
             pltpu.VMEM((n_z, 8, 128), F32),
-            pltpu.VMEM((half, 8, 128), F32),
+            pltpu.VMEM((half // 2 + 1, 8, 128), F32),
             pltpu.VMEM((128, 128), BF16),
             pltpu.VMEM((half, 16, width), BF16),
             pltpu.VMEM((n_dp, half, 32, width), BF16),
             pltpu.VMEM((n_dp, half * 32, hidden), BF16),
             pltpu.VMEM((half, 32, width), BF16),
             pltpu.VMEM((half, 32, width), BF16),
-            pltpu.VMEM((half + 1, tokens, width), BF16),
-            pltpu.VMEM((half, tokens, width), BF16),
-            pltpu.VMEM((2, 2 * tokens, width), F32),
+            pltpu.VMEM((half // 2 + 1, tokens, width), BF16),
+            pltpu.VMEM((half // 2, tokens, width), BF16),
+            pltpu.VMEM((2 * tokens, width), F32),
             pltpu.VMEM((tokens, width), F32),
             pltpu.VMEM((tokens, width), BF16),
-            pltpu.VMEM((half, tokens, width), BF16),
-            pltpu.VMEM((half, tokens, width), BF16),
+            pltpu.VMEM((2, half // 2, 16, width), BF16),
+            pltpu.VMEM((2, half // 2, 16, width), BF16),
+            pltpu.VMEM((2, half // 2, 16, width), BF16),
+            pltpu.VMEM((2, half // 2, 16, width), BF16),
             dma((2,)),
-            dma, dma((2, half, CHUNKS)),
-            dma, dma((2, half)),
+            dma, dma((2, half // 2, CHUNKS)),
+            dma, dma((2, half // 2)),
+            dma, dma((2, half // 2)),
             dma, dma((half // 2,)),
             dma, dma((2, half // 2)),
             dma, dma((2, half // 2)),
@@ -436,8 +459,8 @@
             dma, dma((2, GROUPS)),
             dma, dma((4, GROUPS)),
             dma, dma((GROUPS,)),
-            dma, dma((2, half, CHUNKS)),
-            dma, dma((2, half)),
+            dma, dma((2, half // 2, CHUNKS)),
+            dma, dma((2, half // 2)),
             dma, dma,
         ],
         compiler_params=pltpu.CompilerParams(

time: 144 us -> 131 us (0.910)
  Pallas kernels: 141 us -> 128 us
    pallas_call x1, Pallas kernels: 141 us -> 128 us  [body(): pl.pallas_call(functools.partial(kernel, n_dp, n_exp), out_shape=jax.Shap...]
where the time goes in v3:
time: 131 us
  Pallas kernels  128 us (98%)
  local copies, waits for them, and re-layouts  2.78 us (2%)
    pallas_call x1, Pallas kernels, body(): pl.pallas_call(functools.partial(kernel, n_dp, n_exp), out_shape=jax.Shap...  128 us

profile of v3, /device:TPU:2, one launch (start us, length us, event | category | flops | bytes accessed | tf_op | source)
XLA Modules:
  0.0 131.2 jit_solution(356819858946473181)
XLA Ops:
  0.0 1.3 broadcast_in_dim.6.gain_ref
  1.3 128.4 %shard_map.64 = bf16[64,512]{1,0:T(8,128)(2,1)} custom-call(bf16[64,4096]{1,0:T(8,128)(2,1)} %bitcast.12, s32[8,64]{1,0:T(8,128)} %bitcast.14, f32[8,64]{1,0:T(8,128)} %bitcast.15, bf16[1,4096]{1,0:T(2,128)(2,1)} %broadcast_in_dim.6.gain_ref, bf16[2,192,4096]{2,1,0:T(8,128)(2,1)} %bitcast.10, bf16[1536,512]{1,0:T(8,128)(2,1)} %bitcast.11), custom_call_target="tpu_custom_call" | custom-call | tf_op jit(solution)/shard_map/pallas_call | solution.py:424
  129.8 1.5 %copy.8 = bf16[1,64,512]{2,1,0:T(8,128)(2,1)} copy(bf16[1,64,512]{2,1,0:T(8,128)(2,1)} %bitcast.13) | data formatting | bytes 131072

commit v4 on v3

--- a/solution.py
+++ b/solution.py
@@ -9,7 +9,7 @@
 
 MESH = pl.DeviceIdType.MESH
 F32, BF16 = jnp.float32, jnp.bfloat16
-CHUNKS = 2
+CHUNKS = 4
 GROUPS = 4
 
 
@@ -54,7 +54,7 @@
     wide = x_ref[...].astype(F32)
     scale = lax.rsqrt(jnp.mean(wide * wide, axis=-1, keepdims=True) + 1e-06)
     mine = pl.ds(pl.multiple_of(dp * width, width), width)
-    blk[z] = (x_ref[:, mine].astype(F32) * scale * gain_ref[:, mine].astype(F32)).astype(BF16)
+    blk[z] = (x_ref[:, mine].astype(F32) * scale * gain_ref[mine].astype(F32)[None]).astype(BF16)
     mt[z, :, 0:64] = routes_ref[...].astype(F32)
     mt[z, :, 64:128] = gates_ref[...]
     a_tok = lax.broadcasted_iota(jnp.int32, (128, 128), 0)
@@ -273,17 +273,18 @@
             total = a if total is None else total + a
         eo[p0:p0 + span] = total.astype(BF16).reshape(span, 32, width)
         rr[p0:p0 + span, 0:16, :] = eo[p0:p0 + span, 0:16, :]
-        remote(
-            eo.at[p0:p0 + span, 16:32], rr.at[p0:p0 + span, 16:32], yb_s, yb_r.at[g], ynb
-        ).start()
-
-    def swapped(g):
-        p0 = group_at(g)
-        there = rr.at[p0:p0 + span, 16:32]
-        remote(there, there, yb_s, yb_r.at[g], ynb).wait_recv()
-
-    def leaves_send(g):
-        for p in range(group_at(g), group_at(g) + span, 2):
+        for at in (1, 0):
+            cut = slice(p0 + at * span // 2, p0 + (at + 1) * span // 2)
+            remote(eo.at[cut, 16:32], rr.at[cut, 16:32], yb_s, yb_r.at[at, g], ynb).start()
+
+    def swapped(g, at):
+        p0 = group_at(g) + at * span // 2
+        there = rr.at[p0:p0 + span // 2, 16:32]
+        remote(there, there, yb_s, yb_r.at[at, g], ynb).wait_recv()
+
+    def leaves_send(g, at):
+        p0 = group_at(g) + at * span // 2
+        for p in range(p0, p0 + span // 2, 2):
             j = p // 2
             res = rr[p].astype(F32)
             bout[0, j] = jnp.concatenate([res[0:8], res[16:24]], axis=0).astype(BF16)
@@ -337,12 +338,14 @@
 
     def back_pair(g):
         j = (GROUPS - g) * span // 2
-        swapped(g)
-        leaves_send(g)
+        swapped(g, 1)
+        leaves_send(g, 1)
         ct[...] = share(j, True, g > 0)
         if g == 0:
             oc[...] = ct[tokens:, :] + x_ref[:, mine].astype(F32)
         back_step(j)
+        swapped(g, 0)
+        leaves_send(g, 0)
         ct[...] = share(j - 1, True, True)
         return j - 1
 
@@ -390,8 +393,7 @@
         back_wait(0, 0, piece)
         back_wait(1, 0, piece)
         fin[cut, :] = (oc[cut, :] + rbl[0, cut, :].astype(F32) + rbr[0, cut, :].astype(F32)).astype(BF16)
-    last = remote(fin, out_ref, fin_s, fin_r, over)
-    last.start()
+        remote(fin.at[cut], out_ref.at[cut], fin_s, fin_r.at[piece], over).start()
 
     def drained(ref, sem):
         remote(ref, ref, sem, sem, right).wait_send()
@@ -409,7 +411,10 @@
     drained(ys, yb_s)
     drained(blk.at[0:half - 1], rs_s)
     drained(bout, lf_s)
-    last.wait()
+    drained(fin, fin_s)
+    for piece in range(CHUNKS):
+        cut = slice(piece * part, (piece + 1) * part)
+        remote(fin.at[cut], out_ref.at[cut], fin_s, fin_r.at[piece], over).wait_recv()
 
 
 def body(activations, routes, gate_weights, norm_gain, gate_up_weights, down_weights):
@@ -458,15 +463,15 @@
             dma, dma((2, GROUPS)),
             dma, dma((2, GROUPS)),
             dma, dma((4, GROUPS)),
-            dma, dma((GROUPS,)),
+            dma, dma((2, GROUPS)),
             dma, dma((2, half // 2, CHUNKS)),
             dma, dma((2, half // 2)),
-            dma, dma,
+            dma, dma((CHUNKS,)),
         ],
         compiler_params=pltpu.CompilerParams(
             collective_id=0, has_side_effects=True, vmem_limit_bytes=56 * 1024 * 1024
         ),
-    )(activations[0], routes[0].T, gate_weights[0].T, norm_gain[None], gate_up_weights[0], down_weights[0])
+    )(activations[0], routes[0].T, gate_weights[0].T, norm_gain, gate_up_weights[0], down_weights[0])
     return out[None]
 
 

time: 131 us -> 125 us (0.954)
  Pallas kernels: 128 us -> 123 us
    pallas_call x1, Pallas kernels: 128 us -> 123 us  [body(): pl.pallas_call(functools.partial(kernel, n_dp, n_exp), out_shape=jax.Shap...]
    broadcast_in_dim x1 -> x0, local copies, waits for them, and re-layouts: 1.31 us -> none  [body(): norm_gain[None]]
where the time goes in v4:
time: 125 us
  Pallas kernels  123 us (98%)
  local copies, waits for them, and re-layouts  1.47 us (1%)
    pallas_call x1, Pallas kernels, body(): pl.pallas_call(functools.partial(kernel, n_dp, n_exp), out_shape=jax.Shap...  123 us

profile of v4, /device:TPU:2, one launch (start us, length us, event | category | flops | bytes accessed | tf_op | source)
XLA Modules:
  0.0 124.5 jit_solution(7217256628359342451)
XLA Ops:
  0.0 123.1 %shard_map.64 = bf16[64,512]{1,0:T(8,128)(2,1)} custom-call(bf16[64,4096]{1,0:T(8,128)(2,1)} %bitcast.12, s32[8,64]{1,0:T(8,128)} %bitcast.14, f32[8,64]{1,0:T(8,128)} %bitcast.15, bf16[4096]{0:T(1024)(128)(2,1)} %gain_ref.1, bf16[2,192,4096]{2,1,0:T(8,128)(2,1)} %bitcast.10, bf16[1536,512]{1,0:T(8,128)(2,1)} %bitcast.11), custom_call_target="tpu_custom_call" | custom-call | tf_op jit(solution)/shard_map/pallas_call | solution.py:429
  123.1 1.5 %copy.8 = bf16[1,64,512]{2,1,0:T(8,128)(2,1)} copy(bf16[1,64,512]{2,1,0:T(8,128)(2,1)} %bitcast.13) | data formatting | bytes 131072
